TPU v7x, 512 devices: a whole 4x4x16 slice. The times are simulated.
512 devices in a mesh: seq: 64 (over z, y), tp: 8 (over x, core).
Axes of the slice: x: 4, y: 4, z: 16, core: 2. Of those that a mesh axis runs over, the one named last changes fastest.
Arguments:
- hidden: bfloat16 [384, 2048], P(None, 'seq'), may hold values from -12 to 12
- ln1_gain: float32 [2048], P('seq'), may hold values from 0.1 to 1.9
- wq: bfloat16 [2048, 2048], P('seq', 'tp'), may hold values from -0.125 to 0.125
- wk: bfloat16 [2048, 1024], P('seq', 'tp'), may hold values from -0.125 to 0.125
- wv: bfloat16 [2048, 1024], P('seq', 'tp'), may hold values from -0.125 to 0.125
- wg: bfloat16 [2048, 2048], P('seq', 'tp'), may hold values from -0.125 to 0.125
- q_gain: float32 [128], replicated, may hold values from 1 to 30
- key_gain: float32 [128], replicated, may hold values from 0.5 to 1.5
- wo: bfloat16 [2048, 2048], P('tp', 'seq'), may hold values from -0.5 to 0.5
- ln2_gain: float32 [2048], P('seq'), may hold values from 0.1 to 1.9
- w_gate: bfloat16 [2048, 6144], P('seq', 'tp'), may hold values from -0.125 to 0.125
- w_up: bfloat16 [2048, 6144], P('seq', 'tp'), may hold values from -0.125 to 0.125
- w_down: bfloat16 [6144, 2048], P('tp', 'seq'), may hold values from -0.078125 to 0.078125
- last_gain: float32 [2048], P('seq'), may hold values from 0.1 to 1.9
- head_weight: bfloat16 [2048, 131072], P(None, ('seq', 'tp')), may hold values from -0.125 to 0.125
- inv_temp: float32 [8], replicated, may hold values from 0.5 to 64
- key_cache: bfloat16 [8, 16384, 1024], P(None, 'seq', 'tp'), may hold values from -40 to 40
- value_cache: bfloat16 [8, 16384, 1024], P(None, 'seq', 'tp'), may hold values from -6 to 6
- lengths: int32 [8], replicated, may hold values from 1 to 16336
- parents: int32 [8, 48], replicated, may hold values from 0 to 46, as said below
- accepted: int32 [8], replicated, may hold values from 0 to 47
Outputs:
- logprobs: float32 [384, 131072], P(None, ('seq', 'tp'))
- next_hidden: bfloat16 [384, 2048], P(None, 'seq')
- updated_key_cache: bfloat16 [8, 16384, 1024], P(None, 'seq', 'tp')
- updated_value_cache: bfloat16 [8, 16384, 1024], P(None, 'seq', 'tp')
Inputs may be any that keep to these rules, and one draw needn't show every extreme that they name: parents[r, 0] = 0; for i >= 1, i - 4 <= parents[r, i] < i.
All inputs are finite; a program needn't handle non-finite values.
Results may differ from a plain program's by a relative error of at most 0.012.
Values may be sent and summed in bfloat16 or wider, within the bound.
No kernel may reach another device: no remote copies, remote signals or barrier semaphores. Data moves between devices by JAX's collectives and lax.ppermute only.
A program may use at most 128 MiB of HBM per device.

v0:
```python
import jax
import jax.numpy as jnp
from jax import lax
from jax.sharding import PartitionSpec as P

EPSILON = 1e-06
ROPE_BASE = 1000000.0
NEGATIVE = -1e30


def ancestry(parents):
    node_count = parents.shape[-1]
    node_ids = jnp.arange(node_count, dtype=jnp.int32)
    reachable = (parents[..., :, None] == node_ids[None, :]).astype(jnp.float32)
    reachable = jnp.maximum(reachable, jnp.eye(node_count, dtype=jnp.float32))
    for turn in range((node_count - 1).bit_length()):
        reachable = jnp.minimum(
            jnp.einsum("rij,rjk->rik", reachable, reachable, precision=lax.Precision.HIGHEST), 1.0
        )
    return reachable


def head_norm(values, gain):
    meansq = jnp.mean(values * values, axis=-1, keepdims=True)
    return values * lax.rsqrt(meansq + EPSILON) * gain


def apply_rotary(values, places):
    half_dim = values.shape[-1] // 2
    spread = ROPE_BASE ** (-jnp.arange(half_dim, dtype=jnp.float32) / half_dim)
    angles = places.astype(jnp.float32)[:, None] * spread[None, :]
    cosine = jnp.cos(angles)[:, None, :]
    sine = jnp.sin(angles)[:, None, :]
    lower_part = values[..., :half_dim]
    upper_part = values[..., half_dim:]
    return jnp.concatenate(
        [lower_part * cosine - upper_part * sine, upper_part * cosine + lower_part * sine], axis=-1
    )


def cache_part(query_blocks, key_block, value_block, valid_slot):
    scores = jnp.einsum(
        "rikgd,rckd->rkgic", query_blocks, key_block, preferred_element_type=jnp.float32
    )
    valid_slot = valid_slot[:, None, None, None, :]
    row_peak = jnp.max(jnp.where(valid_slot, scores, NEGATIVE), axis=-1)
    weights = jnp.where(valid_slot, jnp.exp(scores - row_peak[..., None]), 0.0)
    row_mass = jnp.sum(weights, axis=-1)
    weighted = jnp.einsum(
        "rkgic,rckd->rkgid",
        weights.astype(jnp.bfloat16),
        value_block,
        preferred_element_type=jnp.float32,
    )
    return (row_peak, row_mass, weighted)


def on_device(
    hidden,
    ln1_gain,
    wq,
    wk,
    wv,
    wg,
    q_gain,
    key_gain,
    wo,
    ln2_gain,
    w_gate,
    w_up,
    w_down,
    last_gain,
    head_weight,
    inv_temp,
    key_cache,
    value_cache,
    lengths,
    parents,
    accepted,
):
    seq_count = lax.axis_size("seq")
    model_width = hidden.shape[1] * seq_count
    head_dim = q_gain.shape[0]
    query_heads = wq.shape[1] // head_dim
    kv_heads = wk.shape[1] // head_dim
    query_group_size = query_heads // kv_heads
    requests, tree_size = parents.shape
    token_count = hidden.shape[0]
    slot_count = key_cache.shape[1]
    slot_start = lax.axis_index("seq") * slot_count
    parent_links = ancestry(parents)
    tree_node_depth = jnp.sum((parent_links > 0.5).astype(jnp.int32), axis=-1) - 1
    token_position = (lengths[:, None] + tree_node_depth).reshape(-1)
    hidden_wide = hidden.astype(jnp.float32)
    squares = lax.psum(jnp.sum(hidden_wide * hidden_wide, axis=1), "seq")
    normed1 = (hidden_wide * lax.rsqrt(squares / model_width + EPSILON)[:, None] * ln1_gain).astype(
        jnp.bfloat16
    )
    q_sum, key_sum, v_sum, gate = lax.psum(
        (
            jnp.dot(normed1, wq, preferred_element_type=jnp.float32),
            jnp.dot(normed1, wk, preferred_element_type=jnp.float32),
            jnp.dot(normed1, wv, preferred_element_type=jnp.float32),
            jnp.dot(normed1, wg, preferred_element_type=jnp.float32),
        ),
        "seq",
    )
    query_rows_all = apply_rotary(
        head_norm(q_sum.reshape(token_count, query_heads, head_dim), q_gain), token_position
    ) * head_dim ** (-0.5)
    query_rows_all = query_rows_all.astype(jnp.bfloat16).reshape(
        requests, tree_size, kv_heads, query_group_size, head_dim
    )
    draft_keys = apply_rotary(
        head_norm(key_sum.reshape(token_count, kv_heads, head_dim), key_gain), token_position
    ).astype(jnp.bfloat16)
    draft_values = v_sum.astype(jnp.bfloat16)
    tree_keys = draft_keys.reshape(requests, tree_size, kv_heads, head_dim)
    tree_values = draft_values.reshape(requests, tree_size, kv_heads, head_dim)
    cache_keys = key_cache.reshape(requests, slot_count, kv_heads, head_dim)
    cache_values = value_cache.reshape(requests, slot_count, kv_heads, head_dim)
    slot_ids = slot_start + jnp.arange(slot_count, dtype=jnp.int32)
    local_state = cache_part(
        query_rows_all, cache_keys, cache_values, slot_ids[None, :] < lengths[:, None]
    )
    local_peak, local_mass, local_sum = local_state
    cache_peak = lax.pmax(local_peak, "seq")
    factor = jnp.exp(local_peak - cache_peak)
    cache_mass, cache_sum = lax.psum((local_mass * factor, local_sum * factor[..., None]), "seq")
    tree_scores = jnp.einsum(
        "rikgd,rjkd->rkgij", query_rows_all, tree_keys, preferred_element_type=jnp.float32
    )
    valid_node = (parent_links > 0.5)[:, None, None, :, :]
    row_top = jnp.maximum(
        cache_peak, jnp.max(jnp.where(valid_node, tree_scores, NEGATIVE), axis=-1)
    )
    tree_weights = jnp.where(valid_node, jnp.exp(tree_scores - row_top[..., None]), 0.0)
    cache_factor = jnp.exp(cache_peak - row_top)
    row_mass = cache_mass * cache_factor + jnp.sum(tree_weights, axis=-1)
    weighted = cache_sum * cache_factor[..., None] + jnp.einsum(
        "rkgij,rjkd->rkgid",
        tree_weights.astype(jnp.bfloat16),
        tree_values,
        preferred_element_type=jnp.float32,
    )
    attention_result = jnp.transpose(weighted / row_mass[..., None], (0, 3, 1, 2, 4)).reshape(
        token_count, query_heads * head_dim
    )
    gated = (attention_result * jax.nn.sigmoid(gate)).astype(jnp.bfloat16)
    attn_sum = lax.psum(jnp.dot(gated, wo, preferred_element_type=jnp.float32), "tp")
    middle = (hidden_wide + attn_sum).astype(jnp.bfloat16)
    middle_wide = middle.astype(jnp.float32)
    squares_mid = lax.psum(jnp.sum(middle_wide * middle_wide, axis=1), "seq")
    normed2 = (
        middle_wide * lax.rsqrt(squares_mid / model_width + EPSILON)[:, None] * ln2_gain
    ).astype(jnp.bfloat16)
    gate_part, up_part = lax.psum(
        (
            jnp.dot(normed2, w_gate, preferred_element_type=jnp.float32),
            jnp.dot(normed2, w_up, preferred_element_type=jnp.float32),
        ),
        "seq",
    )
    activated = (jax.nn.silu(gate_part) * up_part).astype(jnp.bfloat16)
    down_part = jnp.dot(activated, w_down, preferred_element_type=jnp.float32)
    down_sum = lax.psum(down_part, "tp")
    next_hidden = (middle_wide + down_sum).astype(jnp.bfloat16)
    next_wide = next_hidden.astype(jnp.float32)
    squares_last = lax.psum(jnp.sum(next_wide * next_wide, axis=1), "seq")
    normed3 = (
        next_wide * lax.rsqrt(squares_last / model_width + EPSILON)[:, None] * last_gain
    ).astype(jnp.bfloat16)
    logits = jnp.dot(
        lax.all_gather(normed3, "seq", axis=1, tiled=True),
        head_weight,
        preferred_element_type=jnp.float32,
    )
    logits = logits * jnp.repeat(inv_temp, tree_size)[:, None]
    vocab_top = lax.pmax(jnp.max(logits, axis=1), ("seq", "tp"))
    vocab_total = lax.psum(jnp.sum(jnp.exp(logits - vocab_top[:, None]), axis=1), ("seq", "tp"))
    logprobs = logits - (vocab_top + jnp.log(vocab_total))[:, None]
    accepted_rows = parent_links[jnp.arange(requests), accepted]
    target = token_position.reshape(requests, tree_size)
    slot_all = slot_start + jnp.arange(slot_count, dtype=jnp.int32)
    placed = (slot_all[None, :, None] == target[:, None, :]).astype(jnp.float32) * accepted_rows[
        :, None, :
    ]
    hits = (jnp.sum(placed, axis=2) > 0.5)[:, :, None]
    placed_low = placed.astype(jnp.bfloat16)
    moved_keys = jnp.einsum(
        "rca,rae->rce",
        placed_low,
        draft_keys.reshape(requests, tree_size, kv_heads * head_dim),
        preferred_element_type=jnp.float32,
    ).astype(jnp.bfloat16)
    moved_values = jnp.einsum(
        "rca,rae->rce",
        placed_low,
        draft_values.reshape(requests, tree_size, kv_heads * head_dim),
        preferred_element_type=jnp.float32,
    ).astype(jnp.bfloat16)
    updated_key_cache = jnp.where(hits, moved_keys, key_cache)
    updated_value_cache = jnp.where(hits, moved_values, value_cache)
    return (logprobs, next_hidden, updated_key_cache, updated_value_cache)


def solution(mesh):
    in_specs = (
        P(None, "seq"),
        P("seq"),
        P("seq", "tp"),
        P("seq", "tp"),
        P("seq", "tp"),
        P("seq", "tp"),
        P(),
        P(),
        P("tp", "seq"),
        P("seq"),
        P("seq", "tp"),
        P("seq", "tp"),
        P("tp", "seq"),
        P("seq"),
        P(None, ("seq", "tp")),
        P(),
        P(None, "seq", "tp"),
        P(None, "seq", "tp"),
        P(),
        P(),
        P(),
    )
    out_specs = (P(None, ("seq", "tp")), P(None, "seq"), P(None, "seq", "tp"), P(None, "seq", "tp"))
    return jax.shard_map(
        on_device, mesh=mesh, in_specs=in_specs, out_specs=out_specs, check_vma=False
    )
```

profile of v0, /device:TPU:1, one launch (start us, length us, event | category | flops | bytes accessed | tf_op | source)
XLA Modules:
  0.0 1792.0 jit_solution(4256023891018787633)
XLA Ops:
  7.2 0.8 fusion.51
  8.1 122.9 %psum.98 = f32[384]{0:T(512)S(1)} all-reduce(f32[384]{0:T(512)S(1)} %fusion.51), channel_id=1, replica_groups=mesh['seq'=64,'tp'=8] {'seq'}, use_global_device_ids=true, to_apply=%region_1.0 | all-reduce | flops 384 | bytes 3072 | tf_op jit(solution)/shard_map/psum | solution.py:95
  130.9 1.8 fusion.88
  132.8 1.4 convolution_minimum_fusion.5
  136.2 1.0 fusion.86
  137.7 1.1 fusion.82
  138.7 269.0 %all-reduce.8.cloned.1.call-done = f32[384,2,128]{0,2,1:T(8,128)} async-done(((f32[384,2,128]{0,2,1:T(8,128)}), f32[384,2,128]{0,2,1:T(8,128)}) %all-reduce.8.cloned.1.call-update) | async-done | bytes 393232 | tf_op jit(solution)/shard_map/psum | solution.py:99
  407.7 1.0 multiply_reduce_fusion
  408.8 1.1 multiply_multiply_fusion
  411.8 114.2 %pmax.14 = f32[8,1,2,48]{3,2,0,1:T(2,128)S(1)} all-reduce(f32[8,1,2,48]{3,2,0,1:T(2,128)S(1)} %bitcast.134), channel_id=1, replica_groups=mesh['seq'=64,'tp'=8] {'seq'}, use_global_device_ids=true, to_apply=%region_6.0 | all-reduce | flops 768 | bytes 6144 | tf_op jit(solution)/shard_map/pmax | solution.py:127
  526.5 1.1 fusion.2
  528.0 219.4 %all-reduce.13 = (bf16[384,128]{1,0:T(8,128)(2,1)S(1)}, f32[8,1,2,48]{3,2,0,1:T(2,128)S(1)}) all-reduce(f32[384,128]{1,0:T(8,128)S(1)} %fusion.84, f32[8,1,2,48]{3,2,0,1:T(2,128)S(1)} %get-tuple-element.32), channel_id=1, replica_groups=mesh['seq'=64,'tp'=8] {'seq'}, use_global_device_ids=true, to_apply=%region_11.12 | all-reduce | flops 49920 | bytes 301056 | tf_op jit(solution)/shard_map/psum | solution.py:99
  747.3 74.5 %all-reduce.12.cloned.1.call-done = (f32[8,1,2,48,128]{4,3,2,0,1:T(8,128)}, f32[384,128]{1,0:T(8,128)}, f32[384,256]{1,0:T(8,128)}) async-done(((f32[8,1,2,48,128]{4,3,2,0,1:T(8,128)}, f32[384,128]{1,0:T(8,128)}, f32[384,256]{1,0:T(8,128)}), (f32[8,1,2,48,128]{4,3,2,0,1:T(8,128)}, f32[384,128]{1,0:T(8,128)}, f32[384,256]{1,0:T(8,128)})) %all-reduce.12.cloned.1.call-update) | async-done | bytes 983056 | tf_op jit(solution)/shard_map/psum | solution.py:129
  821.8 1.1 multiply_reduce_fusion.1
  822.9 1.1 multiply_bitcast_fusion
  824.0 0.8 fusion.25
  826.7 39.8 %psum.105 = f32[384,32]{0,1:T(8,128)S(1)} all-reduce(f32[384,32]{0,1:T(8,128)S(1)} %fusion.43), channel_id=1, replica_groups=mesh['seq'=64,'tp'=8] {'tp'}, use_global_device_ids=true, to_apply=%region_16.17 | all-reduce | flops 12288 | bytes 98304 | tf_op jit(solution)/shard_map/psum | solution.py:150
  866.5 110.1 %psum.106 = f32[384]{0:T(512)S(1)} all-reduce(f32[384]{0:T(512)S(1)} %get-tuple-element.21), channel_id=1, replica_groups=mesh['seq'=64,'tp'=8] {'seq'}, use_global_device_ids=true, to_apply=%region_18.19 | all-reduce | flops 384 | bytes 3072 | tf_op jit(solution)/shard_map/psum | solution.py:153
  976.7 1.4 fusion.63
  978.1 1.4 fusion.65
  979.6 295.4 %all-reduce.10.cloned.1.call-done = (f32[384,768]{1,0:T(8,128)}, f32[384,768]{1,0:T(8,128)}) async-done(((f32[384,768]{1,0:T(8,128)}, f32[384,768]{1,0:T(8,128)}), (f32[384,768]{1,0:T(8,128)}, f32[384,768]{1,0:T(8,128)})) %all-reduce.10.cloned.1.call-update) | async-done | bytes 2359312 | tf_op jit(solution)/shard_map/psum | solution.py:157
  1275.1 2.1 fusion.8
  1277.2 30.1 %psum.109 = f32[384,32]{0,1:T(8,128)S(1)} all-reduce(f32[384,32]{0,1:T(8,128)S(1)} %fusion.8), channel_id=1, replica_groups=mesh['seq'=64,'tp'=8] {'tp'}, use_global_device_ids=true, to_apply=%region_21.22 | all-reduce | flops 12288 | bytes 98304 | tf_op jit(solution)/shard_map/psum | solution.py:166
  1307.3 112.8 %psum.110 = f32[384]{0:T(512)S(1)} all-reduce(f32[384]{0:T(512)S(1)} %get-tuple-element.19), channel_id=1, replica_groups=mesh['seq'=64,'tp'=8] {'seq'}, use_global_device_ids=true, to_apply=%region_23.24 | all-reduce | flops 384 | bytes 3072 | tf_op jit(solution)/shard_map/psum | solution.py:169
  1420.1 0.7 fusion.50
  1421.9 1.7 fusion.1
  1423.5 1.6 fusion
  1425.1 148.8 %all-gather.2.cloned.1.call-done = bf16[384,2048]{0,1:T(8,128)(2,1)} async-done(((bf16[384,32]{0,1:T(8,128)(2,1)}), bf16[384,2048]{0,1:T(8,128)(2,1)}) %all-gather.2.cloned.1.call-update) | async-done | bytes 1572880 | tf_op jit(solution)/shard_map/all_gather | solution.py:174
  1573.9 2.2 fusion.93
  1576.1 109.6 %pmax.15 = f32[384]{0:T(512)S(1)} all-reduce(f32[384]{0:T(512)S(1)} %get-tuple-element.41), channel_id=1, replica_groups=mesh['seq'=64,'tp'=8] {'seq','tp'}, use_global_device_ids=true, to_apply=%region_25.26 | all-reduce | flops 384 | bytes 3072 | tf_op jit(solution)/shard_map/pmax | solution.py:179
  1685.8 98.8 %psum.111 = f32[384]{0:T(512)S(1)} all-reduce(f32[384]{0:T(512)S(1)} %exponential_reduce_fusion), channel_id=1, replica_groups=mesh['seq'=64,'tp'=8] {'seq','tp'}, use_global_device_ids=true, to_apply=%region_27.28 | all-reduce | flops 384 | bytes 3072 | tf_op jit(solution)/shard_map/psum | solution.py:180
  1784.6 0.9 copy.35
  (100 shorter events, 8.2 us)
Async XLA Ops:
  7.2 1566.7 %copy-start = (bf16[2048,256]{1,0:T(8,128)(2,1)S(1)}, bf16[2048,256]{1,0:T(8,128)(2,1)}, u32[]{:S(2)}) copy-start(bf16[2048,256]{1,0:T(8,128)(2,1)} %param.35) | copy-start | bytes 3145732
  7.2 400.6 %all-reduce.8.cloned.1.call-start = ((), (), s32[]{:S(2)}) async-start(), calls=%async_computation | async-start | bytes 786432 | tf_op jit(solution)/shard_map/psum | solution.py:99
  132.7 689.1 %all-reduce.12.cloned.1.call-start = ((), (), s32[]{:S(2)}) async-start(), calls=%async_computation.3 | async-start | bytes 1966080 | tf_op jit(solution)/shard_map/psum | solution.py:129
  134.6 1.4 copy-start.12
  134.6 1.6 copy-start.1
  134.6 1.6 copy-start.8
  134.6 1.6 copy-start.9
  135.0 2.7 copy-start.7
  135.3 273.5 %copy-start.16 = (f32[128]{0:T(128)S(1)}, f32[128]{0:T(128)}, u32[]{:S(2)}) copy-start(f32[128]{0:T(128)} %param.27) | copy-start | bytes 1540
  410.4 1.0 copy-start.2
  411.4 115.0 %copy-start.3 = (bf16[8,256,128]{2,1,0:T(8,128)(2,1)S(1)}, bf16[8,256,128]{2,1,0:T(8,128)(2,1)}, u32[]{:S(2)}) copy-start(bf16[8,256,128]{2,1,0:T(8,128)(2,1)} %param.38) | copy-start | bytes 1572868
  526.5 1.2 copy-start.10
  527.6 295.3 %copy-start.13 = (f32[128]{0:T(128)S(1)}, f32[128]{0:T(128)}, u32[]{:S(2)}) copy-start(f32[128]{0:T(128)} %param.28) | copy-start | bytes 1540
  527.6 747.5 %all-reduce.10.cloned.1.call-start = ((), (), s32[]{:S(2)}) async-start(), calls=%async_computation.2 | async-start | bytes 4718592 | tf_op jit(solution)/shard_map/psum | solution.py:157
  822.9 2.5 copy-start.18
  825.4 1.0 copy-start.17
  825.4 1.0 copy-start.20
  826.0 150.7 %copy-start.5 = (bf16[32,768]{1,0:T(8,128)(2,1)S(1)}, bf16[32,768]{1,0:T(8,128)(2,1)}, u32[]{:S(2)}) copy-start(bf16[32,768]{1,0:T(8,128)(2,1)} %param.32) | copy-start | bytes 147460
  826.0 150.7 %copy-start.11 = (f32[32]{0:T(128)S(1)}, f32[32]{0:T(128)}, u32[]{:S(2)}) copy-start(f32[32]{0:T(128)} %param.30) | copy-start | bytes 388
  826.7 151.5 %copy-start.6 = (bf16[32,768]{1,0:T(8,128)(2,1)S(1)}, bf16[32,768]{1,0:T(8,128)(2,1)}, u32[]{:S(2)}) copy-start(bf16[32,768]{1,0:T(8,128)(2,1)} %param.31) | copy-start | bytes 147460
  979.5 295.5 %copy-start.19 = (bf16[768,32]{0,1:T(8,128)(2,1)S(1)}, bf16[768,32]{0,1:T(8,128)(2,1)}, u32[]{:S(2)}) copy-start(bf16[768,32]{0,1:T(8,128)(2,1)} %param.33) | copy-start | bytes 147460
  979.6 594.3 %all-gather.2.cloned.1.call-start = ((), (), s32[]{:S(2)}) async-start(), calls=%async_computation.1 | async-start | bytes 1597440 | tf_op jit(solution)/shard_map/all_gather | solution.py:174
  1275.0 145.0 %copy-start.14 = (f32[32]{0:T(128)S(1)}, f32[32]{0:T(128)}, u32[]{:S(2)}) copy-start(f32[32]{0:T(128)} %param.34) | copy-start | bytes 388
  1275.0 145.7 %copy-start.15 = (f32[8]{0:T(128)S(1)}, f32[8]{0:T(128)}, u32[]{:S(2)}) copy-start(f32[8]{0:T(128)} %param.36) | copy-start | bytes 100
  1275.0 146.0 %copy-start.21 = (s32[8]{0:T(128)S(1)}, s32[8]{0:T(128)}, u32[]{:S(2)}) copy-start(s32[8]{0:T(128)} %param.41) | copy-start | bytes 100
  1307.3 117.8 %copy-start.4 = (bf16[384,32]{0,1:T(8,128)(2,1)}, bf16[384,32]{0,1:T(8,128)(2,1)S(1)}, u32[]{:S(2)}) copy-start(bf16[384,32]{0,1:T(8,128)(2,1)S(1)} %get-tuple-element.20) | copy-start | bytes 73732
Sparse Core Ops, SparseCore 0:
  132.9 274.8 all-reduce.7
  527.7 294.0 all-reduce.11
  979.7 295.2 all-reduce.9
  1420.9 152.9 all-gather.1
where the time goes:
time: 1790 us
  blocking collectives  958 us (54%)
  waiting for transfers between devices  788 us (44%)
  matrix products  19.9 us (1%)
    psum x1, waiting for transfers between devices, on_device(): lax.psum((jnp.dot(normed2, w_gate, preferred_element_type=jnp.float32), j...  295 us
    psum x1, waiting for transfers between devices, on_device(): lax.psum((jnp.dot(normed1, wq, preferred_element_type=jnp.float32), jnp.d...  269 us
    psum x1, blocking collectives, on_device(): lax.psum((jnp.dot(normed1, wq, preferred_element_type=jnp.float32), jnp.d...  219 us
    all_gather x1, waiting for transfers between devices, on_device(): lax.all_gather(normed3, 'seq', axis=1, tiled=True)  149 us
    psum x1, blocking collectives, on_device(): squares = lax.psum(jnp.sum(hidden_wide * hidden_wide, axis=1), 'seq')  123 us
    pmax x1, blocking collectives, on_device(): cache_peak = lax.pmax(local_peak, 'seq')  114 us
    psum x1, blocking collectives, on_device(): squares_last = lax.psum(jnp.sum(next_wide * next_wide, axis=1), 'seq')  113 us
    psum x1, blocking collectives, on_device(): squares_mid = lax.psum(jnp.sum(middle_wide * middle_wide, axis=1), 'seq')  110 us
  transfers between devices with their start and end apart: 4, of which 4 were waited for; matrix products, arithmetic and copies ran while one was open for 1% of the time, Pallas kernels for 0%

commit v1 on v0

--- a/solution.py
+++ b/solution.py
@@ -177,7 +177,9 @@
     )
     logits = logits * jnp.repeat(inv_temp, tree_size)[:, None]
     vocab_top = lax.pmax(jnp.max(logits, axis=1), ("seq", "tp"))
-    vocab_total = lax.psum(jnp.sum(jnp.exp(logits - vocab_top[:, None]), axis=1), ("seq", "tp"))
+    vocab_total = lax.psum(
+        lax.psum(jnp.sum(jnp.exp(logits - vocab_top[:, None]), axis=1), "tp"), "seq"
+    )
     logprobs = logits - (vocab_top + jnp.log(vocab_total))[:, None]
     accepted_rows = parent_links[jnp.arange(requests), accepted]
     target = token_position.reshape(requests, tree_size)

time: 1790 us -> 1850 us (1.034); the launches traced: 1790 us -> 1820 us
  blocking collectives: 958 us -> 984 us
    psum x1 -> x2, blocking collectives: 98.8 us -> 125 us  [the longest x1 112 us: on_device(): lax.psum(lax.psum(jnp.sum(jnp.exp(logits - vocab_top[:, None]), axis=1),...]
where the time goes in v1:
time: 1850 us; the launch traced here: 1820 us
  blocking collectives  984 us (53%)
  waiting for transfers between devices  788 us (43%)
  matrix products  19.9 us (1%)
    psum x1, waiting for transfers between devices, on_device(): lax.psum((jnp.dot(normed2, w_gate, preferred_element_type=jnp.float32), j...  295 us
    psum x1, waiting for transfers between devices, on_device(): lax.psum((jnp.dot(normed1, wq, preferred_element_type=jnp.float32), jnp.d...  269 us
    psum x1, blocking collectives, on_device(): lax.psum((jnp.dot(normed1, wq, preferred_element_type=jnp.float32), jnp.d...  219 us
    all_gather x1, waiting for transfers between devices, on_device(): lax.all_gather(normed3, 'seq', axis=1, tiled=True)  149 us
    psum x1, blocking collectives, on_device(): squares = lax.psum(jnp.sum(hidden_wide * hidden_wide, axis=1), 'seq')  123 us
    pmax x1, blocking collectives, on_device(): cache_peak = lax.pmax(local_peak, 'seq')  114 us
    psum x1, blocking collectives, on_device(): squares_last = lax.psum(jnp.sum(next_wide * next_wide, axis=1), 'seq')  113 us
    psum x1, blocking collectives, on_device(): lax.psum(lax.psum(jnp.sum(jnp.exp(logits - vocab_top[:, None]), axis=1),...  112 us
  transfers between devices with their start and end apart: 4, of which 4 were waited for; matrix products, arithmetic and copies ran while one was open for 1% of the time, Pallas kernels for 0%

profile of v1, /device:TPU:1, one launch (start us, length us, event | category | flops | bytes accessed | tf_op | source)
XLA Modules:
  0.0 1818.2 jit_solution(14181584428916280802)
XLA Ops:
  7.2 0.8 fusion.51
  8.1 122.9 %psum.105 = f32[384]{0:T(512)S(1)} all-reduce(f32[384]{0:T(512)S(1)} %fusion.51), channel_id=1, replica_groups=mesh['seq'=64,'tp'=8] {'seq'}, use_global_device_ids=true, to_apply=%region_1.0 | all-reduce | flops 384 | bytes 3072 | tf_op jit(solution)/shard_map/psum | solution.py:95
  130.9 1.8 fusion.88
  132.8 1.4 convolution_minimum_fusion.5
  136.2 1.0 fusion.86
  137.7 1.1 fusion.82
  138.7 269.0 %all-reduce.8.cloned.1.call-done = f32[384,2,128]{0,2,1:T(8,128)} async-done(((f32[384,2,128]{0,2,1:T(8,128)}), f32[384,2,128]{0,2,1:T(8,128)}) %all-reduce.8.cloned.1.call-update) | async-done | bytes 393232 | tf_op jit(solution)/shard_map/psum | solution.py:99
  407.7 1.0 multiply_reduce_fusion
  408.8 1.1 multiply_multiply_fusion
  411.8 114.2 %pmax.14 = f32[8,1,2,48]{3,2,0,1:T(2,128)S(1)} all-reduce(f32[8,1,2,48]{3,2,0,1:T(2,128)S(1)} %bitcast.134), channel_id=1, replica_groups=mesh['seq'=64,'tp'=8] {'seq'}, use_global_device_ids=true, to_apply=%region_6.0 | all-reduce | flops 768 | bytes 6144 | tf_op jit(solution)/shard_map/pmax | solution.py:127
  526.5 1.1 fusion.2
  528.0 219.4 %all-reduce.13 = (bf16[384,128]{1,0:T(8,128)(2,1)S(1)}, f32[8,1,2,48]{3,2,0,1:T(2,128)S(1)}) all-reduce(f32[384,128]{1,0:T(8,128)S(1)} %fusion.84, f32[8,1,2,48]{3,2,0,1:T(2,128)S(1)} %get-tuple-element.32), channel_id=1, replica_groups=mesh['seq'=64,'tp'=8] {'seq'}, use_global_device_ids=true, to_apply=%region_11.12 | all-reduce | flops 49920 | bytes 301056 | tf_op jit(solution)/shard_map/psum | solution.py:99
  747.3 74.5 %all-reduce.12.cloned.1.call-done = (f32[8,1,2,48,128]{4,3,2,0,1:T(8,128)}, f32[384,128]{1,0:T(8,128)}, f32[384,256]{1,0:T(8,128)}) async-done(((f32[8,1,2,48,128]{4,3,2,0,1:T(8,128)}, f32[384,128]{1,0:T(8,128)}, f32[384,256]{1,0:T(8,128)}), (f32[8,1,2,48,128]{4,3,2,0,1:T(8,128)}, f32[384,128]{1,0:T(8,128)}, f32[384,256]{1,0:T(8,128)})) %all-reduce.12.cloned.1.call-update) | async-done | bytes 983056 | tf_op jit(solution)/shard_map/psum | solution.py:129
  821.8 1.1 multiply_reduce_fusion.1
  822.9 1.1 multiply_bitcast_fusion
  824.0 0.8 fusion.25
  826.7 39.8 %psum.112 = f32[384,32]{0,1:T(8,128)S(1)} all-reduce(f32[384,32]{0,1:T(8,128)S(1)} %fusion.43), channel_id=1, replica_groups=mesh['seq'=64,'tp'=8] {'tp'}, use_global_device_ids=true, to_apply=%region_16.17 | all-reduce | flops 12288 | bytes 98304 | tf_op jit(solution)/shard_map/psum | solution.py:150
  866.5 110.1 %psum.113 = f32[384]{0:T(512)S(1)} all-reduce(f32[384]{0:T(512)S(1)} %get-tuple-element.21), channel_id=1, replica_groups=mesh['seq'=64,'tp'=8] {'seq'}, use_global_device_ids=true, to_apply=%region_18.19 | all-reduce | flops 384 | bytes 3072 | tf_op jit(solution)/shard_map/psum | solution.py:153
  976.7 1.4 fusion.63
  978.1 1.4 fusion.65
  979.6 295.4 %all-reduce.10.cloned.1.call-done = (f32[384,768]{1,0:T(8,128)}, f32[384,768]{1,0:T(8,128)}) async-done(((f32[384,768]{1,0:T(8,128)}, f32[384,768]{1,0:T(8,128)}), (f32[384,768]{1,0:T(8,128)}, f32[384,768]{1,0:T(8,128)})) %all-reduce.10.cloned.1.call-update) | async-done | bytes 2359312 | tf_op jit(solution)/shard_map/psum | solution.py:157
  1275.1 2.1 fusion.8
  1277.2 30.1 %psum.116 = f32[384,32]{0,1:T(8,128)S(1)} all-reduce(f32[384,32]{0,1:T(8,128)S(1)} %fusion.8), channel_id=1, replica_groups=mesh['seq'=64,'tp'=8] {'tp'}, use_global_device_ids=true, to_apply=%region_21.22 | all-reduce | flops 12288 | bytes 98304 | tf_op jit(solution)/shard_map/psum | solution.py:166
  1307.3 112.8 %psum.117 = f32[384]{0:T(512)S(1)} all-reduce(f32[384]{0:T(512)S(1)} %get-tuple-element.19), channel_id=1, replica_groups=mesh['seq'=64,'tp'=8] {'seq'}, use_global_device_ids=true, to_apply=%region_23.24 | all-reduce | flops 384 | bytes 3072 | tf_op jit(solution)/shard_map/psum | solution.py:169
  1421.9 1.7 fusion.1
  1423.5 1.6 fusion
  1425.1 148.8 %all-gather.2.cloned.1.call-done = bf16[384,2048]{0,1:T(8,128)(2,1)} async-done(((bf16[384,32]{0,1:T(8,128)(2,1)}), bf16[384,2048]{0,1:T(8,128)(2,1)}) %all-gather.2.cloned.1.call-update) | async-done | bytes 1572880 | tf_op jit(solution)/shard_map/all_gather | solution.py:174
  1573.9 2.2 fusion.93
  1576.1 109.6 %pmax.15 = f32[384]{0:T(512)S(1)} all-reduce(f32[384]{0:T(512)S(1)} %get-tuple-element.41), channel_id=1, replica_groups=mesh['seq'=64,'tp'=8] {'seq','tp'}, use_global_device_ids=true, to_apply=%region_25.26 | all-reduce | flops 384 | bytes 3072 | tf_op jit(solution)/shard_map/pmax | solution.py:179
  1685.8 12.4 psum.118
  1698.2 112.5 %psum.119 = f32[384]{0:T(512)S(1)} all-reduce(f32[384]{0:T(512)S(1)} %psum.118), channel_id=1, replica_groups=mesh['seq'=64,'tp'=8] {'seq'}, use_global_device_ids=true, to_apply=%region_28.29 | all-reduce | flops 384 | bytes 3072 | tf_op jit(solution)/shard_map/psum | solution.py:180
  1810.7 0.9 copy.35
  (101 shorter events, 8.8 us)
Async XLA Ops:
  7.2 1566.7 %copy-start = (bf16[2048,256]{1,0:T(8,128)(2,1)S(1)}, bf16[2048,256]{1,0:T(8,128)(2,1)}, u32[]{:S(2)}) copy-start(bf16[2048,256]{1,0:T(8,128)(2,1)} %param.35) | copy-start | bytes 3145732
  7.2 400.6 %all-reduce.8.cloned.1.call-start = ((), (), s32[]{:S(2)}) async-start(), calls=%async_computation | async-start | bytes 786432 | tf_op jit(solution)/shard_map/psum | solution.py:99
  132.7 689.1 %all-reduce.12.cloned.1.call-start = ((), (), s32[]{:S(2)}) async-start(), calls=%async_computation.3 | async-start | bytes 1966080 | tf_op jit(solution)/shard_map/psum | solution.py:129
  134.6 1.4 copy-start.12
  134.6 1.6 copy-start.1
  134.6 1.6 copy-start.8
  134.6 1.6 copy-start.9
  135.0 2.7 copy-start.7
  135.3 273.5 %copy-start.16 = (f32[128]{0:T(128)S(1)}, f32[128]{0:T(128)}, u32[]{:S(2)}) copy-start(f32[128]{0:T(128)} %param.27) | copy-start | bytes 1540
  410.4 1.0 copy-start.2
  411.4 115.0 %copy-start.3 = (bf16[8,256,128]{2,1,0:T(8,128)(2,1)S(1)}, bf16[8,256,128]{2,1,0:T(8,128)(2,1)}, u32[]{:S(2)}) copy-start(bf16[8,256,128]{2,1,0:T(8,128)(2,1)} %param.38) | copy-start | bytes 1572868
  526.5 1.2 copy-start.10
  527.6 295.3 %copy-start.13 = (f32[128]{0:T(128)S(1)}, f32[128]{0:T(128)}, u32[]{:S(2)}) copy-start(f32[128]{0:T(128)} %param.28) | copy-start | bytes 1540
  527.6 747.5 %all-reduce.10.cloned.1.call-start = ((), (), s32[]{:S(2)}) async-start(), calls=%async_computation.2 | async-start | bytes 4718592 | tf_op jit(solution)/shard_map/psum | solution.py:157
  822.9 2.5 copy-start.18
  825.4 1.0 copy-start.17
  825.4 1.0 copy-start.20
  826.0 150.7 %copy-start.5 = (bf16[32,768]{1,0:T(8,128)(2,1)S(1)}, bf16[32,768]{1,0:T(8,128)(2,1)}, u32[]{:S(2)}) copy-start(bf16[32,768]{1,0:T(8,128)(2,1)} %param.32) | copy-start | bytes 147460
  826.0 150.7 %copy-start.11 = (f32[32]{0:T(128)S(1)}, f32[32]{0:T(128)}, u32[]{:S(2)}) copy-start(f32[32]{0:T(128)} %param.30) | copy-start | bytes 388
  826.7 151.5 %copy-start.6 = (bf16[32,768]{1,0:T(8,128)(2,1)S(1)}, bf16[32,768]{1,0:T(8,128)(2,1)}, u32[]{:S(2)}) copy-start(bf16[32,768]{1,0:T(8,128)(2,1)} %param.31) | copy-start | bytes 147460
  979.5 295.5 %copy-start.19 = (bf16[768,32]{0,1:T(8,128)(2,1)S(1)}, bf16[768,32]{0,1:T(8,128)(2,1)}, u32[]{:S(2)}) copy-start(bf16[768,32]{0,1:T(8,128)(2,1)} %param.33) | copy-start | bytes 147460
  979.6 594.3 %all-gather.2.cloned.1.call-start = ((), (), s32[]{:S(2)}) async-start(), calls=%async_computation.1 | async-start | bytes 1597440 | tf_op jit(solution)/shard_map/all_gather | solution.py:174
  1275.0 145.0 %copy-start.14 = (f32[32]{0:T(128)S(1)}, f32[32]{0:T(128)}, u32[]{:S(2)}) copy-start(f32[32]{0:T(128)} %param.34) | copy-start | bytes 388
  1275.0 145.7 %copy-start.15 = (f32[8]{0:T(128)S(1)}, f32[8]{0:T(128)}, u32[]{:S(2)}) copy-start(f32[8]{0:T(128)} %param.36) | copy-start | bytes 100
  1275.0 146.0 %copy-start.21 = (s32[8]{0:T(128)S(1)}, s32[8]{0:T(128)}, u32[]{:S(2)}) copy-start(s32[8]{0:T(128)} %param.41) | copy-start | bytes 100
  1307.3 117.8 %copy-start.4 = (bf16[384,32]{0,1:T(8,128)(2,1)}, bf16[384,32]{0,1:T(8,128)(2,1)S(1)}, u32[]{:S(2)}) copy-start(bf16[384,32]{0,1:T(8,128)(2,1)S(1)} %get-tuple-element.20) | copy-start | bytes 73732
Sparse Core Ops, SparseCore 0:
  132.9 274.8 all-reduce.7
  527.7 294.0 all-reduce.11
  979.7 295.2 all-reduce.9
  1420.9 152.9 all-gather.1
